TPU v7x, 128 devices: a whole 4x4x4 slice. The times are simulated.
128 devices in a mesh: req: 8 (over x, core), exp: 16 (over y, z).
Axes of the slice: x: 4, y: 4, z: 4, core: 2. Of those that a mesh axis runs over, the one named last changes fastest.
Arguments:
- queries: bfloat16 [8192, 2048], P('req', 'exp'), may hold values from -6 to 6
- keys: bfloat16 [8192, 2048], P('req', 'exp'), may hold values from -15 to 15
- values: bfloat16 [8192, 2048], P('req', 'exp'), may hold values from -6 to 6
- prefix_keys: bfloat16 [4, 4096, 2048], P(None, 'req', 'exp'), may hold values from -15 to 15
- prefix_values: bfloat16 [4, 4096, 2048], P(None, 'req', 'exp'), may hold values from -6 to 6
- lengths: int32 [8, 8], P('req'), may hold values from 1 to 512, 1024 in all within a row
- groups: int32 [8, 8], P('req'), may hold values from 0 to 3
- residual: bfloat16 [8192, 2048], P(('req', 'exp')), may hold values from -6 to 6
- out_proj: bfloat16 [2048, 2048], P('exp'), may hold values from -0.125 to 0.125
- norm_gain: bfloat16 [2048], replicated, may hold values from 0.099609375 to 1.8984375
- expert_ids: int32 [8192, 4], P(('req', 'exp')), may hold values from 0 to 31, all different within a row; in each aligned block of 64 rows (0 to 63, 64 to 127, ...) at most 16 rows name the same one
- expert_gates: bfloat16 [8192, 4], P(('req', 'exp')), may hold values from 0.049804688 to 0.5
- w_gate: bfloat16 [32, 2048, 704], P('exp'), may hold values from -0.125 to 0.125
- w_up: bfloat16 [32, 2048, 704], P('exp'), may hold values from -0.125 to 0.125
- w_down: bfloat16 [32, 704, 2048], P('exp'), may hold values from -0.21875 to 0.21875
Outputs:
- layer_out: bfloat16 [8192, 2048], P(('req', 'exp'))
Inputs may be any that keep to these rules, and one draw needn't show every extreme that they name: The 8 lengths of a row sum to 1024; the longest request of each row has half of 1024 tokens. `expert_ids`: each row names 4 different experts. Among the 64 tokens of one device, no expert is named more than 16 times; on some device some expert is named exactly 16 times.
All inputs are finite; a program needn't handle non-finite values.
Results may differ from a plain program's by a relative error of at most 0.02.
Values may be sent and summed in bfloat16 or wider, within the bound.
A program may use at most 256 MiB of HBM per device.

v0:
```python
import math
import jax
import jax.numpy as jnp
from jax import lax
from jax.sharding import PartitionSpec as P

HEAD = 128
TOPK = 4
EXPERTS = 32
G = 4
RQ = 8
ROW_TOK = 1024
NEG = -1e30


def token_layout(lengths, groups):
    req_ends = jnp.cumsum(lengths, axis=-1)
    starts = req_ends - lengths
    position = jnp.arange(ROW_TOK, dtype=jnp.int32)
    request = jnp.sum((position[None, :, None] >= req_ends[:, None, :]).astype(jnp.int32), axis=-1)
    onehot = request[:, :, None] == jnp.arange(RQ, dtype=jnp.int32)[None, None, :]
    first_tok = jnp.sum(jnp.where(onehot, starts[:, None, :], 0), axis=-1)
    tok_group = jnp.sum(jnp.where(onehot, groups[:, None, :], 0), axis=-1)
    return (request, position[None, :] - first_tok, tok_group)


def split_blocks(row_count):
    if row_count % 1024 == 0 and row_count > 1024:
        return row_count // 1024
    return 1


def pack_parts(parts):
    return jnp.concatenate([parts[0], parts[1], parts[2]], axis=1)


def unpack_parts(packed, head_count):
    columns = head_count * HEAD
    return (
        packed[:, :columns],
        packed[:, columns : columns + head_count],
        packed[:, columns + head_count :],
    )


def attend_prefix(query_rows, query_group, prefix_k, prefix_v):
    row_count, columns = query_rows.shape
    head_count = columns // HEAD
    span = prefix_k.shape[1]
    key_grid = prefix_k.reshape(G, span, head_count, HEAD)
    val_grid = prefix_v.reshape(G, span, head_count, HEAD)
    blocks = split_blocks(row_count)
    block_len = row_count // blocks
    scaling = 1.0 / math.sqrt(HEAD)

    def per_block(pieces):
        block_q, block_g = pieces
        query_grid = block_q.reshape(block_len, head_count, HEAD)
        scores = (
            jnp.einsum("qhd,gkhd->hqgk", query_grid, key_grid, preferred_element_type=jnp.float32)
            * scaling
        )
        member = block_g[:, None] == jnp.arange(G, dtype=jnp.int32)[None, :]
        scores = jnp.where(member[None, :, :, None], scores, NEG)
        maxima = jnp.max(scores, axis=(2, 3))
        exp_terms = jnp.exp(scores - maxima[:, :, None, None])
        totals = jnp.sum(exp_terms, axis=(2, 3))
        weighted = jnp.einsum(
            "hqgk,gkhd->qhd",
            exp_terms.astype(jnp.bfloat16),
            val_grid,
            preferred_element_type=jnp.float32,
        )
        return (weighted.reshape(block_len, columns), maxima.T, totals.T)

    weighted, maxima, totals = lax.map(
        per_block,
        (query_rows.reshape(blocks, block_len, columns), query_group.reshape(blocks, block_len)),
    )
    return (
        weighted.reshape(row_count, columns),
        maxima.reshape(row_count, head_count),
        totals.reshape(row_count, head_count),
    )


def attend_suffix(queries, keys, values, request, position):
    row_count, columns = queries.shape
    head_count = columns // HEAD
    blocks = split_blocks(row_count)
    block_len = row_count // blocks
    scaling = 1.0 / math.sqrt(HEAD)
    key_grid = keys.reshape(row_count, head_count, HEAD)
    val_grid = values.reshape(row_count, head_count, HEAD)

    def per_block(pieces):
        block_q, block_req, block_pos = pieces
        query_grid = block_q.reshape(block_len, head_count, HEAD)
        scores = (
            jnp.einsum("qhd,khd->hqk", query_grid, key_grid, preferred_element_type=jnp.float32)
            * scaling
        )
        allowed = (request[None, :] == block_req[:, None]) & (
            position[None, :] <= block_pos[:, None]
        )
        scores = jnp.where(allowed[None, :, :], scores, NEG)
        maxima = jnp.max(scores, axis=2)
        exp_terms = jnp.exp(scores - maxima[:, :, None])
        totals = jnp.sum(exp_terms, axis=2)
        weighted = jnp.einsum(
            "hqk,khd->qhd",
            exp_terms.astype(jnp.bfloat16),
            val_grid,
            preferred_element_type=jnp.float32,
        )
        return (weighted.reshape(block_len, columns), maxima.T, totals.T)

    weighted, maxima, totals = lax.map(
        per_block,
        (
            queries.reshape(blocks, block_len, columns),
            request.reshape(blocks, block_len),
            position.reshape(blocks, block_len),
        ),
    )
    return (
        weighted.reshape(row_count, columns),
        maxima.reshape(row_count, head_count),
        totals.reshape(row_count, head_count),
    )


def combine(former, latter):
    weighted_a, maxima_a, totals_a = former
    weighted_b, maxima_b, totals_b = latter
    row_count, head_count = maxima_a.shape
    maxima = jnp.maximum(maxima_a, maxima_b)
    factor_a = jnp.exp(maxima_a - maxima)
    factor_b = jnp.exp(maxima_b - maxima)
    weighted = (
        weighted_a.reshape(row_count, head_count, HEAD) * factor_a[:, :, None]
        + weighted_b.reshape(row_count, head_count, HEAD) * factor_b[:, :, None]
    )
    return (
        weighted.reshape(row_count, head_count * HEAD),
        maxima,
        totals_a * factor_a + totals_b * factor_b,
    )


def per_device(
    queries,
    keys,
    values,
    prefix_keys,
    prefix_values,
    lengths,
    groups,
    residual,
    out_proj,
    norm_gain,
    expert_ids,
    expert_gates,
    w_gate,
    w_up,
    w_down,
):
    row_tok, columns = queries.shape
    head_count = columns // HEAD
    tok_dev = residual.shape[0]
    request, position, tok_group = token_layout(lengths, groups)
    request, position, tok_group = (request[0], position[0], tok_group[0])
    all_groups = lax.all_gather(tok_group, "req", axis=0, tiled=True)
    partial_value = pack_parts(
        attend_prefix(
            lax.all_gather(queries, "req", axis=0, tiled=True),
            all_groups,
            prefix_keys,
            prefix_values,
        )
    )
    returned = lax.all_to_all(partial_value, "req", split_axis=0, concat_axis=0, tiled=True)
    owners = returned.shape[0] // row_tok
    back_w, back_m, back_t = unpack_parts(returned, head_count)
    all_weighted = back_w.reshape(owners, row_tok, head_count, HEAD)
    all_maxima = back_m.reshape(owners, row_tok, head_count)
    all_totals = back_t.reshape(owners, row_tok, head_count)
    maxima = jnp.max(all_maxima, axis=0)
    factor = jnp.exp(all_maxima - maxima[None])
    weighted = jnp.sum(all_weighted * factor[..., None], axis=0).reshape(row_tok, columns)
    prefix_part = (weighted, maxima, jnp.sum(all_totals * factor, axis=0))
    suffix_part = attend_suffix(queries, keys, values, request, position)
    weighted, maxima, totals = combine(prefix_part, suffix_part)
    attended = (
        (weighted.reshape(row_tok, head_count, HEAD) / totals[:, :, None])
        .reshape(row_tok, columns)
        .astype(jnp.bfloat16)
    )
    projected = lax.psum_scatter(
        jnp.dot(attended, out_proj, preferred_element_type=jnp.float32),
        "exp",
        scatter_dimension=0,
        tiled=True,
    )
    stream = residual.astype(jnp.float32) + projected
    meansq = jnp.mean(stream * stream, axis=-1, keepdims=True)
    normed = (stream * lax.rsqrt(meansq + 1e-06) * norm_gain.astype(jnp.float32)).astype(
        jnp.bfloat16
    )
    capacity = max(2, tok_dev // 4)
    flat_ids = expert_ids.reshape(-1)
    onehot = (flat_ids[:, None] == jnp.arange(EXPERTS, dtype=jnp.int32)[None, :]).astype(jnp.int32)
    slot_of = jnp.sum(onehot * (jnp.cumsum(onehot, axis=0) - 1), axis=1)
    source_rows = jnp.arange(tok_dev * TOPK, dtype=jnp.int32) // TOPK
    buffer = (
        jnp.zeros((EXPERTS, capacity, normed.shape[1]), jnp.bfloat16)
        .at[flat_ids, slot_of]
        .set(normed[source_rows])
    )
    exp_count = lax.axis_size("exp")
    exp_dev = w_gate.shape[0]
    received = lax.all_to_all(buffer, "exp", split_axis=0, concat_axis=0, tiled=True)
    slots = received.shape[1]
    grid_in = received.reshape(exp_count, exp_dev, slots, received.shape[2])
    gate_h = jnp.einsum("secd,edf->secf", grid_in, w_gate, preferred_element_type=jnp.float32)
    up_h = jnp.einsum("secd,edf->secf", grid_in, w_up, preferred_element_type=jnp.float32)
    hidden = (jax.nn.silu(gate_h) * up_h).astype(jnp.bfloat16)
    expert_out = jnp.einsum("secf,efd->secd", hidden, w_down, preferred_element_type=jnp.float32)
    returned = lax.all_to_all(
        expert_out.reshape(EXPERTS, slots, received.shape[2]),
        "exp",
        split_axis=0,
        concat_axis=0,
        tiled=True,
    )
    gathered = returned[flat_ids, slot_of] * expert_gates.reshape(-1).astype(jnp.float32)[:, None]
    mixture = jnp.sum(gathered.reshape(tok_dev, TOPK, gathered.shape[1]), axis=1)
    return (stream + mixture).astype(jnp.bfloat16)


def solution(mesh):
    in_specs = (
        P("req", "exp"),
        P("req", "exp"),
        P("req", "exp"),
        P(None, "req", "exp"),
        P(None, "req", "exp"),
        P("req", None),
        P("req", None),
        P(("req", "exp"), None),
        P("exp", None),
        P(),
        P(("req", "exp"), None),
        P(("req", "exp"), None),
        P("exp", None, None),
        P("exp", None, None),
        P("exp", None, None),
    )
    out_specs = P(("req", "exp"), None)
    return jax.shard_map(
        per_device, mesh=mesh, in_specs=in_specs, out_specs=out_specs, check_vma=False
    )
```

profile of v0, /device:TPU:0, one launch (start us, length us, event | category | flops | bytes accessed | tf_op | source)
XLA Modules:
  0.0 431.7 jit_solution(6236507258747720294)
XLA Ops:
  9.6 13.3 %all_gather.6 = s32[8192]{0:T(1024)S(1)} all-gather(s32[1024]{0:T(1024)S(1)} %get-tuple-element.81), channel_id=1, replica_groups=mesh['req'=8,'exp'=16] {'req'}, dimensions={0}, use_global_device_ids=true | all-gather | bytes 36864 | tf_op jit(solution)/shard_map/all_gather | solution.py:173
  22.9 13.8 %all-gather.2.cloned.1.call-done = bf16[8192,128]{1,0:T(8,128)(2,1)} async-done(((bf16[1024,128]{1,0:T(8,128)(2,1)}), bf16[8192,128]{1,0:T(8,128)(2,1)}) %all-gather.2.cloned.1.call-update) | async-done | bytes 2097168 | tf_op jit(solution)/shard_map/all_gather | solution.py:176
  36.7 55.2 %while.2 = (s32[]{:T(128)}, f32[8,1024,128]{1,2,0:T(8,128)}, f32[8,1024,1]{1,2,0:T(1,128)S(1)}, f32[8,1024,1]{1,2,0:T(1,128)S(1)}, s32[8,1024]{1,0:T(8,128)S(1)}...) while((s32[]{:T(128)}, f32[8,1024,128]{1,2,0:T(8,128)}, ...), condition=%wide.region_6.7_spmd, body=%wide.region_3.6_spmd.sunk | while | flops 1096812544 | bytes 29160576 | solution.py:76
  36.7 2.4 fusion.99
  39.1 1.7 fusion.101
  40.9 2.7 fusion.100
  43.6 2.4 fusion.99
  46.0 1.7 fusion.101
  47.7 2.7 fusion.100
  50.5 2.4 fusion.99
  52.9 1.7 fusion.101
  54.7 2.8 fusion.100
  57.4 2.4 fusion.99
  59.8 1.7 fusion.101
  61.6 2.7 fusion.100
  64.3 2.4 fusion.99
  66.7 1.7 fusion.101
  68.5 2.7 fusion.100
  71.2 2.4 fusion.99
  73.6 1.7 fusion.101
  75.4 2.7 fusion.100
  78.1 2.4 fusion.99
  80.5 1.7 fusion.101
  82.3 2.7 fusion.100
  85.0 2.4 fusion.99
  87.4 1.7 fusion.101
  89.2 2.8 fusion.100
  91.9 4.9 %pad_maximum_fusion = f32[8,1024,130]{1,2,0:T(8,128)} fusion(f32[8,1024,1]{1,2,0:T(1,128)S(1)} %get-tuple-element.78, f32[8,1024,1]{1,2,0:T(1,128)S(1)} %get-tuple-element.77, f32[8,1024,128]{1,2,0:T(8,128)} %get-tuple-element.76), kind=kLoop, calls=%fused_computation.30 | loop fusion | flops 2129920 | bytes 8519680 | tf_op jit(solution)/shard_map/concatenate | solution.py:34
  96.9 4.7 %all-to-all-start = ((f32[8,1024,130]{1,2,0:T(8,128)}), f32[8,1024,130]{1,2,0:T(8,128)}, u32[]{:S(2)}, u32[]{:S(2)}) async-start(f32[8,1024,130]{1,2,0:T(8,128)} %pad_maximum_fusion), calls=%async_computation | async-start | bytes 8912896 | tf_op jit(solution)/shard_map/all_to_all | solution.py:182
  103.2 2.0 copy-done.1
  105.8 48.2 %all-to-all-done = f32[8,1024,130]{1,2,0:T(8,128)} async-done(((f32[8,1024,130]{1,2,0:T(8,128)}), f32[8,1024,130]{1,2,0:T(8,128)}, u32[]{:S(2)}, u32[]{:S(2)}) %all-to-all-start) | async-done | bytes 4259872 | tf_op jit(solution)/shard_map/all_to_all | solution.py:182
  154.1 4.7 %copy.101 = f32[8,1024,130]{1,0,2:T(8,128)S(1)} copy(f32[8,1024,130]{1,2,0:T(8,128)} %all-to-all-done) | data formatting | bytes 8519680 | tf_op jit(solution)/shard_map/all_to_all | solution.py:182
  159.1 3.9 copy.89
  163.2 2.3 slice.26
  165.6 5.6 %copy.90 = f32[16,8,8,1024]{3,2,1,0:T(8,128)S(1)} copy(f32[16,8,8,1024]{3,1,2,0:T(8,128)} %bitcast.182) | data formatting | bytes 8388608
  173.0 8.2 %fusion.71 = f32[1024,2048]{1,0:T(8,128)} fusion(bf16[128,2048]{1,0:T(8,128)(2,1)S(1)} %copy-done, bf16[1024,128]{1,0:T(8,128)(2,1)S(1)} %copy-done.5, f32[1024,1024]{0,1:T(8,128)} %copy-done.1, f32[1024]{0:T(1024)S(1)} %get-tuple-element.109, f32[1024,128]{1,0:T(8,128)S(1)} %copy.68, f32[1024]{0:T(1024)S(1)} %get-tuple-element.99, ...), kind=kOutput, calls=%fused_computation.58 | convolution fusion | flops 808058880 | bytes 13910016 | tf_op jit(solution)/shard_map/dot_general | solution.py:200
  183.3 82.6 %reduce-scatter.2.cloned.1.call-done = f32[64,2048]{1,0:T(8,128)} async-done(((f32[1024,2048]{1,0:T(8,128)}), f32[64,2048]{1,0:T(8,128)}) %reduce-scatter.2.cloned.1.call-update) | async-done | bytes 524304 | tf_op jit(solution)/shard_map/reduce_scatter | solution.py:199
  268.3 2.3 gather_fusion
  270.9 33.3 %scatter_fusion = bf16[32,16,2048]{2,1,0:T(8,128)(2,1)S(1)} fusion(bf16[32,16,2048]{2,1,0:T(8,128)(2,1)S(1)} %broadcast_in_dim.105, s32[256]{0:T(256)S(1)} %bitcast.180, bf16[256,2048]{1,0:T(8,128)(2,1)} %gather_fusion), kind=kCustom, calls=%fused_computation.2 | custom fusion | bytes 3147776 | tf_op jit(solution)/shard_map/scatter | solution.py:218
  304.2 32.2 %all_to_all.19 = bf16[32,16,2048]{2,1,0:T(8,128)(2,1)S(1)} all-to-all(bf16[32,16,2048]{2,1,0:T(8,128)(2,1)S(1)} %scatter_fusion), channel_id=1, replica_groups=mesh['req'=8,'exp'=16] {'exp'}, dimensions={0} | all-to-all | bytes 4194304 | tf_op jit(solution)/shard_map/all_to_all | solution.py:222
  337.7 4.5 %fusion.24 = f32[2,16,16,704]{3,2,1,0:T(8,128)S(1)} fusion(bf16[2,2048,704]{1,2,0:T(8,128)(2,1)} %param.29, bf16[16,2,16,2048]{3,2,1,0:T(8,128)(2,1)S(1)} %bitcast.184), kind=kOutput, calls=%fused_computation.28 | convolution fusion | flops 1476395008 | bytes 9306112 | tf_op jit(solution)/shard_map/secd,edf->secf/dot_general | solution.py:225
  342.1 10.6 %fusion.29 = f32[16,2,16,2048]{3,2,0,1:T(8,128)} fusion(bf16[2,704,2048]{2,1,0:T(8,128)(2,1)} %param.31, f32[2,16,16,704]{3,2,1,0:T(8,128)S(1)} %fusion.24, bf16[2,2048,704]{1,2,0:T(8,128)(2,1)} %param.30, bf16[16,2,16,2048]{3,2,1,0:T(8,128)(2,1)} %bitcast.185), kind=kOutput, calls=%fused_computation.38 | convolution fusion | flops 2954952704 | bytes 19267584 | tf_op jit(solution)/shard_map/secf,efd->secd/dot_general | solution.py:228
  352.7 4.7 %copy.75 = f32[16,2,16,2048]{3,2,1,0:T(8,128)} copy(f32[16,2,16,2048]{3,2,0,1:T(8,128)} %fusion.29) | data formatting | bytes 8388608 | tf_op jit(solution)/shard_map/secf,efd->secd/transpose | solution.py:228
  357.4 4.7 %all-to-all-start.2 = ((f32[32,16,2048]{2,1,0:T(8,128)}), f32[32,16,2048]{2,1,0:T(8,128)}, u32[]{:S(2)}, u32[]{:S(2)}) async-start(f32[32,16,2048]{2,1,0:T(8,128)} %bitcast.183), calls=%async_computation.3 | async-start | bytes 8388608 | tf_op jit(solution)/shard_map/all_to_all | solution.py:229
  362.2 52.8 %all-to-all-done.2 = f32[32,16,2048]{2,1,0:T(8,128)} async-done(((f32[32,16,2048]{2,1,0:T(8,128)}), f32[32,16,2048]{2,1,0:T(8,128)}, u32[]{:S(2)}, u32[]{:S(2)}) %all-to-all-start.2) | async-done | bytes 4194336 | tf_op jit(solution)/shard_map/all_to_all | solution.py:229
  415.0 4.0 gather_fusion.1
  419.0 1.7 gather.10
  420.7 3.2 multiply_reduce_fusion
  (107 shorter events, 14.7 us)
Async XLA Ops:
  6.5 166.4 %copy-start = (bf16[128,2048]{1,0:T(8,128)(2,1)S(1)}, bf16[128,2048]{1,0:T(8,128)(2,1)}, u32[]{:S(2)}) copy-start(bf16[128,2048]{1,0:T(8,128)(2,1)} %param.25) | copy-start | bytes 1572868
  6.5 30.2 %all-gather.2.cloned.1.call-start = ((), (), s32[]{:S(2)}) async-start(), calls=%async_computation.4 | async-start | bytes 2359296 | tf_op jit(solution)/shard_map/all_gather | solution.py:176
  39.1 1.7 copy-start.10
  46.0 1.7 copy-start.10
  52.9 1.7 copy-start.10
  59.8 1.7 copy-start.10
  66.7 1.7 copy-start.10
  73.6 1.7 copy-start.10
  80.5 1.7 copy-start.10
  87.4 1.7 copy-start.10
  96.9 5.2 %copy-start.6 = (bf16[1024,128]{1,0:T(8,128)(2,1)S(1)}, bf16[1024,128]{1,0:T(8,128)(2,1)}, u32[]{:S(2)}) copy-start(bf16[1024,128]{1,0:T(8,128)(2,1)} %param.17) | copy-start | bytes 786436
  96.9 5.3 %copy-start.11 = (bf16[1024,128]{1,0:T(8,128)(2,1)S(1)}, bf16[1024,128]{1,0:T(8,128)(2,1)}, u32[]{:S(2)}) copy-start(bf16[1024,128]{1,0:T(8,128)(2,1)} %param.18) | copy-start | bytes 786436
  96.9 57.2 %all-to-all-start = ((f32[8,1024,130]{1,2,0:T(8,128)}), f32[8,1024,130]{1,2,0:T(8,128)}, u32[]{:S(2)}, u32[]{:S(2)}) async-start(f32[8,1024,130]{1,2,0:T(8,128)} %pad_maximum_fusion), calls=%async_computation | async-start | bytes 8912896 | tf_op jit(solution)/shard_map/all_to_all | solution.py:182
  101.6 164.3 %reduce-scatter.2.cloned.1.call-start = ((), (), s32[]{:S(2)}) async-start(), calls=%async_computation.5 | async-start | bytes 8912896 | tf_op jit(solution)/shard_map/reduce_scatter | solution.py:199
  103.2 2.0 copy-start.1
  171.2 1.7 copy-start.5
  181.2 0.7 copy-start.8
  181.2 1.1 copy-start.7
  181.2 84.7 %copy-start.3 = (bf16[64,2048]{1,0:T(8,128)(2,1)S(1)}, bf16[64,2048]{1,0:T(8,128)(2,1)}, u32[]{:S(2)}) copy-start(bf16[64,2048]{1,0:T(8,128)(2,1)} %param.24) | copy-start | bytes 786436
  336.3 1.3 copy-start.4
  357.4 4.7 %copy-start.9 = (bf16[64,4]{0,1:T(4,128)(2,1)S(1)}, bf16[64,4]{0,1:T(4,128)(2,1)}, u32[]{:S(2)}) copy-start(bf16[64,4]{0,1:T(4,128)(2,1)} %param.28) | copy-start | bytes 1540
  357.4 57.6 %all-to-all-start.2 = ((f32[32,16,2048]{2,1,0:T(8,128)}), f32[32,16,2048]{2,1,0:T(8,128)}, u32[]{:S(2)}, u32[]{:S(2)}) async-start(f32[32,16,2048]{2,1,0:T(8,128)} %bitcast.183), calls=%async_computation.3 | async-start | bytes 8388608 | tf_op jit(solution)/shard_map/all_to_all | solution.py:229
  419.0 4.9 %copy-start.2 = (f32[64,2048]{1,0:T(8,128)S(1)}, f32[64,2048]{1,0:T(8,128)}, u32[]{:S(2)}) copy-start(f32[64,2048]{1,0:T(8,128)} %reduce-scatter.2.cloned.1.call-done) | copy-start | bytes 1572868
Sparse Core Ops, SparseCore 0:
  9.1 27.5 all-gather.1
  181.3 84.5 reduce-scatter.1
where the time goes:
time: 438 us; the launch traced here: 432 us
  waiting for transfers between devices  198 us (45%)
  local copies, waits for them, and re-layouts  68.4 us (16%)
  matrix products  65.4 us (15%)
  blocking collectives  45.4 us (10%)
  other arithmetic  30.3 us (7%)
  between operations  14 us (3%)
  starting transfers between devices  9.88 us (2%)
    reduce_scatter x1, waiting for transfers between devices, per_device(): lax.psum_scatter(jnp.dot(attended, out_proj, preferred_element_type=jnp.f...  82.6 us
    all_to_all x1, waiting for transfers between devices, per_device(): lax.all_to_all(expert_out.reshape(EXPERTS, slots, received.shape[2]), 'ex...  52.8 us
    all_to_all x1, waiting for transfers between devices, per_device(): lax.all_to_all(partial_value, 'req', split_axis=0, concat_axis=0, tiled=T...  48.2 us
    scatter x1, local copies, waits for them, and re-layouts, per_device(): buffer = jnp.zeros((EXPERTS, capacity, normed.shape[1]), jnp.bfloat16).at...  33.3 us
    all_to_all x1, blocking collectives, per_device(): lax.all_to_all(buffer, 'exp', split_axis=0, concat_axis=0, tiled=True)  32.2 us
    dot_general x8, matrix products, per_block(): jnp.einsum('hqgk,gkhd->qhd', exp_terms.astype(jnp.bfloat16), val_grid, pr...  21.9 us
    dot_general x8, matrix products, per_block(): jnp.einsum('qhd,gkhd->hqgk', query_grid, key_grid, preferred_element_type...  19.1 us
    unnamed x26, local copies, waits for them, and re-layouts  13.9 us
  transfers between devices with their start and end apart: 4, of which 4 were waited for; matrix products, arithmetic and copies ran while one was open for 1% of the time, Pallas kernels for 0%

commit v1 on v0

--- a/solution.py
+++ b/solution.py
@@ -170,7 +170,12 @@
     tok_dev = residual.shape[0]
     request, position, tok_group = token_layout(lengths, groups)
     request, position, tok_group = (request[0], position[0], tok_group[0])
-    all_groups = lax.all_gather(tok_group, "req", axis=0, tiled=True)
+    ring = [tok_group]
+    for hop in range(7):
+        ring.append(lax.ppermute(ring[-1], "req", [(dev, (dev + 1) % 8) for dev in range(8)]))
+    all_groups = jnp.roll(
+        jnp.concatenate(ring[::-1], axis=0), (lax.axis_index("req") + 1) * ring[0].shape[0], axis=0
+    )
     partial_value = pack_parts(
         attend_prefix(
             lax.all_gather(queries, "req", axis=0, tiled=True),

time: 438 us -> 442 us (level)
  waiting for transfers between devices: 198 us -> 216 us
  blocking collectives: 45.4 us -> 31.9 us
    ppermute x0 -> x7, waiting for transfers between devices: none -> 29.7 us  [per_device(): lax.ppermute(ring[-1], 'req', [(dev, (dev + 1) % 8) for dev in range(8)])]
    all_gather x1, waiting for transfers between devices: 13.8 us -> 0.02 us  [per_device(): lax.all_gather(queries, 'req', axis=0, tiled=True)]
    all_gather x1 -> x0, blocking collectives: 13.3 us -> none  [per_device(): all_groups = lax.all_gather(tok_group, 'req', axis=0, tiled=True)]
    unnamed x26 -> x41, local copies, waits for them, and re-layouts: 13.9 us -> 13.9 us
  transfers between devices with their start and end apart: 4 -> 11, of which waited for: 4 -> 10; matrix products, arithmetic and copies ran while one was open for 1% -> 1% of each run, Pallas kernels for 0% -> 0%
where the time goes in v1:
time: 442 us; the launch traced here: 436 us
  waiting for transfers between devices  216 us (49%)
  local copies, waits for them, and re-layouts  68.5 us (15%)
  matrix products  65.4 us (15%)
  blocking collectives  31.9 us (7%)
  other arithmetic  30.3 us (7%)
  between operations  14.1 us (3%)
  starting transfers between devices  9.91 us (2%)
    reduce_scatter x1, waiting for transfers between devices, per_device(): lax.psum_scatter(jnp.dot(attended, out_proj, preferred_element_type=jnp.f...  84.1 us
    all_to_all x1, waiting for transfers between devices, per_device(): lax.all_to_all(expert_out.reshape(EXPERTS, slots, received.shape[2]), 'ex...  52.9 us
    all_to_all x1, waiting for transfers between devices, per_device(): lax.all_to_all(partial_value, 'req', split_axis=0, concat_axis=0, tiled=T...  48.2 us
    scatter x1, local copies, waits for them, and re-layouts, per_device(): buffer = jnp.zeros((EXPERTS, capacity, normed.shape[1]), jnp.bfloat16).at...  33.3 us
    all_to_all x1, blocking collectives, per_device(): lax.all_to_all(buffer, 'exp', split_axis=0, concat_axis=0, tiled=True)  31.9 us
    ppermute x7, waiting for transfers between devices, per_device(): lax.ppermute(ring[-1], 'req', [(dev, (dev + 1) % 8) for dev in range(8)])  29.7 us
    dot_general x8, matrix products, per_block(): jnp.einsum('hqgk,gkhd->qhd', exp_terms.astype(jnp.bfloat16), val_grid, pr...  21.9 us
    dot_general x8, matrix products, per_block(): jnp.einsum('qhd,gkhd->hqgk', query_grid, key_grid, preferred_element_type...  19.1 us
  transfers between devices with their start and end apart: 11, of which 10 were waited for; matrix products, arithmetic and copies ran while one was open for 1% of the time, Pallas kernels for 0%

profile of v1, /device:TPU:0, one launch (start us, length us, event | category | flops | bytes accessed | tf_op | source)
XLA Modules:
  0.0 435.9 jit_solution(1285087541836410994)
XLA Ops:
  9.6 4.2 collective-permute-done
  13.8 4.2 collective-permute-done.1
  18.1 4.2 collective-permute-done.2
  22.3 4.2 collective-permute-done.3
  26.6 4.2 collective-permute-done.4
  30.8 4.2 collective-permute-done.5
  35.1 4.2 collective-permute-done.6
  39.5 55.3 %while.2 = (s32[]{:T(128)}, f32[8,1024,128]{1,2,0:T(8,128)}, f32[8,1024,1]{1,2,0:T(1,128)S(1)}, f32[8,1024,1]{1,2,0:T(1,128)S(1)}, s32[8,1024]{1,0:T(8,128)S(1)}...) while((s32[]{:T(128)}, f32[8,1024,128]{1,2,0:T(8,128)}, ...), condition=%wide.region_6.7_spmd, body=%wide.region_3.6_spmd.sunk | while | flops 1096812544 | bytes 29160576 | solution.py:76
  39.6 2.4 fusion.99
  42.0 1.7 fusion.101
  43.7 2.7 fusion.100
  46.5 2.4 fusion.99
  48.9 1.7 fusion.101
  50.6 2.7 fusion.100
  53.4 2.4 fusion.99
  57.5 2.8 fusion.100
  60.3 2.4 fusion.99
  64.4 2.7 fusion.100
  67.2 2.4 fusion.99
  69.6 1.7 fusion.101
  71.3 2.7 fusion.100
  74.1 2.4 fusion.99
  78.2 2.7 fusion.100
  81.0 2.4 fusion.99
  85.1 2.7 fusion.100
  87.9 2.4 fusion.99
  90.3 1.7 fusion.101
  92.0 2.8 fusion.100
  94.8 4.9 %pad_maximum_fusion = f32[8,1024,130]{1,2,0:T(8,128)} fusion(f32[8,1024,1]{1,2,0:T(1,128)S(1)} %get-tuple-element.78, f32[8,1024,1]{1,2,0:T(1,128)S(1)} %get-tuple-element.77, f32[8,1024,128]{1,2,0:T(8,128)} %get-tuple-element.76), kind=kLoop, calls=%fused_computation.30 | loop fusion | flops 2129920 | bytes 8519680 | tf_op jit(solution)/shard_map/concatenate | solution.py:34
  99.7 4.7 %all-to-all-start = ((f32[8,1024,130]{1,2,0:T(8,128)}), f32[8,1024,130]{1,2,0:T(8,128)}, u32[]{:S(2)}, u32[]{:S(2)}) async-start(f32[8,1024,130]{1,2,0:T(8,128)} %pad_maximum_fusion), calls=%async_computation | async-start | bytes 8912896 | tf_op jit(solution)/shard_map/all_to_all | solution.py:187
  106.1 2.0 copy-done.1
  108.7 48.2 %all-to-all-done = f32[8,1024,130]{1,2,0:T(8,128)} async-done(((f32[8,1024,130]{1,2,0:T(8,128)}), f32[8,1024,130]{1,2,0:T(8,128)}, u32[]{:S(2)}, u32[]{:S(2)}) %all-to-all-start) | async-done | bytes 4259872 | tf_op jit(solution)/shard_map/all_to_all | solution.py:187
  156.9 4.7 %copy.101 = f32[8,1024,130]{1,0,2:T(8,128)S(1)} copy(f32[8,1024,130]{1,2,0:T(8,128)} %all-to-all-done) | data formatting | bytes 8519680 | tf_op jit(solution)/shard_map/all_to_all | solution.py:187
  162.0 3.9 copy.89
  166.1 2.3 slice.26
  168.5 5.6 %copy.90 = f32[16,8,8,1024]{3,2,1,0:T(8,128)S(1)} copy(f32[16,8,8,1024]{3,1,2,0:T(8,128)} %bitcast.182) | data formatting | bytes 8388608
  175.8 8.2 %fusion.71 = f32[1024,2048]{1,0:T(8,128)} fusion(bf16[128,2048]{1,0:T(8,128)(2,1)S(1)} %copy-done, bf16[1024,128]{1,0:T(8,128)(2,1)S(1)} %copy-done.5, f32[1024,1024]{0,1:T(8,128)} %copy-done.1, f32[1024]{0:T(1024)S(1)} %get-tuple-element.109, f32[1024,128]{1,0:T(8,128)S(1)} %copy.68, f32[1024]{0:T(1024)S(1)} %get-tuple-element.99, ...), kind=kOutput, calls=%fused_computation.58 | convolution fusion | flops 808058880 | bytes 13910016 | tf_op jit(solution)/shard_map/dot_general | solution.py:205
  186.1 84.1 %reduce-scatter.2.cloned.1.call-done = f32[64,2048]{1,0:T(8,128)} async-done(((f32[1024,2048]{1,0:T(8,128)}), f32[64,2048]{1,0:T(8,128)}) %reduce-scatter.2.cloned.1.call-update) | async-done | bytes 524304 | tf_op jit(solution)/shard_map/reduce_scatter | solution.py:204
  272.6 2.3 gather_fusion
  275.2 33.3 %scatter_fusion = bf16[32,16,2048]{2,1,0:T(8,128)(2,1)S(1)} fusion(bf16[32,16,2048]{2,1,0:T(8,128)(2,1)S(1)} %broadcast_in_dim.105, s32[256]{0:T(256)S(1)} %bitcast.180, bf16[256,2048]{1,0:T(8,128)(2,1)} %gather_fusion), kind=kCustom, calls=%fused_computation.2 | custom fusion | bytes 3147776 | tf_op jit(solution)/shard_map/scatter | solution.py:223
  308.5 31.9 %all_to_all.19 = bf16[32,16,2048]{2,1,0:T(8,128)(2,1)S(1)} all-to-all(bf16[32,16,2048]{2,1,0:T(8,128)(2,1)S(1)} %scatter_fusion), channel_id=1, replica_groups=mesh['req'=8,'exp'=16] {'exp'}, dimensions={0} | all-to-all | bytes 4194304 | tf_op jit(solution)/shard_map/all_to_all | solution.py:227
  341.8 4.5 %fusion.24 = f32[2,16,16,704]{3,2,1,0:T(8,128)S(1)} fusion(bf16[2,2048,704]{1,2,0:T(8,128)(2,1)} %param.29, bf16[16,2,16,2048]{3,2,1,0:T(8,128)(2,1)S(1)} %bitcast.184), kind=kOutput, calls=%fused_computation.28 | convolution fusion | flops 1476395008 | bytes 9306112 | tf_op jit(solution)/shard_map/secd,edf->secf/dot_general | solution.py:230
  346.2 10.6 %fusion.29 = f32[16,2,16,2048]{3,2,0,1:T(8,128)} fusion(bf16[2,704,2048]{2,1,0:T(8,128)(2,1)} %param.31, f32[2,16,16,704]{3,2,1,0:T(8,128)S(1)} %fusion.24, bf16[2,2048,704]{1,2,0:T(8,128)(2,1)} %param.30, bf16[16,2,16,2048]{3,2,1,0:T(8,128)(2,1)} %bitcast.185), kind=kOutput, calls=%fused_computation.38 | convolution fusion | flops 2954952704 | bytes 19267584 | tf_op jit(solution)/shard_map/secf,efd->secd/dot_general | solution.py:233
  356.8 4.7 %copy.75 = f32[16,2,16,2048]{3,2,1,0:T(8,128)} copy(f32[16,2,16,2048]{3,2,0,1:T(8,128)} %fusion.29) | data formatting | bytes 8388608 | tf_op jit(solution)/shard_map/secf,efd->secd/transpose | solution.py:233
  361.5 4.7 %all-to-all-start.2 = ((f32[32,16,2048]{2,1,0:T(8,128)}), f32[32,16,2048]{2,1,0:T(8,128)}, u32[]{:S(2)}, u32[]{:S(2)}) async-start(f32[32,16,2048]{2,1,0:T(8,128)} %bitcast.183), calls=%async_computation.3 | async-start | bytes 8388608 | tf_op jit(solution)/shard_map/all_to_all | solution.py:234
  366.3 52.9 %all-to-all-done.2 = f32[32,16,2048]{2,1,0:T(8,128)} async-done(((f32[32,16,2048]{2,1,0:T(8,128)}), f32[32,16,2048]{2,1,0:T(8,128)}, u32[]{:S(2)}, u32[]{:S(2)}) %all-to-all-start.2) | async-done | bytes 4194336 | tf_op jit(solution)/shard_map/all_to_all | solution.py:234
  419.1 4.0 gather_fusion.1
  424.9 3.2 multiply_reduce_fusion
  (137 shorter events, 23.3 us)
Async XLA Ops:
  6.5 169.3 %copy-start = (bf16[128,2048]{1,0:T(8,128)(2,1)S(1)}, bf16[128,2048]{1,0:T(8,128)(2,1)}, u32[]{:S(2)}) copy-start(bf16[128,2048]{1,0:T(8,128)(2,1)} %param.25) | copy-start | bytes 1572868
  6.5 33.0 %all-gather.2.cloned.1.call-start = ((), (), s32[]{:S(2)}) async-start(), calls=%async_computation.4 | async-start | bytes 2359296 | tf_op jit(solution)/shard_map/all_gather | solution.py:181
  9.6 4.3 collective-permute-start
  13.8 4.2 collective-permute-start.1
  18.1 4.2 collective-permute-start.2
  22.3 4.2 collective-permute-start.3
  26.6 4.2 collective-permute-start.4
  30.8 4.2 collective-permute-start.5
  35.1 4.2 collective-permute-start.6
  42.0 1.7 copy-start.10
  48.9 1.7 copy-start.10
  55.8 1.7 copy-start.10
  62.7 1.7 copy-start.10
  69.6 1.7 copy-start.10
  76.5 1.7 copy-start.10
  83.4 1.7 copy-start.10
  90.3 1.7 copy-start.10
  99.7 5.2 %copy-start.6 = (bf16[1024,128]{1,0:T(8,128)(2,1)S(1)}, bf16[1024,128]{1,0:T(8,128)(2,1)}, u32[]{:S(2)}) copy-start(bf16[1024,128]{1,0:T(8,128)(2,1)} %param.17) | copy-start | bytes 786436
  99.7 5.3 %copy-start.11 = (bf16[1024,128]{1,0:T(8,128)(2,1)S(1)}, bf16[1024,128]{1,0:T(8,128)(2,1)}, u32[]{:S(2)}) copy-start(bf16[1024,128]{1,0:T(8,128)(2,1)} %param.18) | copy-start | bytes 786436
  99.7 57.2 %all-to-all-start = ((f32[8,1024,130]{1,2,0:T(8,128)}), f32[8,1024,130]{1,2,0:T(8,128)}, u32[]{:S(2)}, u32[]{:S(2)}) async-start(f32[8,1024,130]{1,2,0:T(8,128)} %pad_maximum_fusion), calls=%async_computation | async-start | bytes 8912896 | tf_op jit(solution)/shard_map/all_to_all | solution.py:187
  104.5 165.8 %reduce-scatter.2.cloned.1.call-start = ((), (), s32[]{:S(2)}) async-start(), calls=%async_computation.5 | async-start | bytes 8912896 | tf_op jit(solution)/shard_map/reduce_scatter | solution.py:204
  106.1 2.0 copy-start.1
  174.1 1.7 copy-start.5
  184.0 0.7 copy-start.8
  184.0 1.1 copy-start.7
  184.0 86.2 %copy-start.3 = (bf16[64,2048]{1,0:T(8,128)(2,1)S(1)}, bf16[64,2048]{1,0:T(8,128)(2,1)}, u32[]{:S(2)}) copy-start(bf16[64,2048]{1,0:T(8,128)(2,1)} %param.24) | copy-start | bytes 786436
  340.4 1.3 copy-start.4
  361.5 4.7 %copy-start.9 = (bf16[64,4]{0,1:T(4,128)(2,1)S(1)}, bf16[64,4]{0,1:T(4,128)(2,1)}, u32[]{:S(2)}) copy-start(bf16[64,4]{0,1:T(4,128)(2,1)} %param.28) | copy-start | bytes 1540
  361.5 57.7 %all-to-all-start.2 = ((f32[32,16,2048]{2,1,0:T(8,128)}), f32[32,16,2048]{2,1,0:T(8,128)}, u32[]{:S(2)}, u32[]{:S(2)}) async-start(f32[32,16,2048]{2,1,0:T(8,128)} %bitcast.183), calls=%async_computation.3 | async-start | bytes 8388608 | tf_op jit(solution)/shard_map/all_to_all | solution.py:234
  423.2 4.9 %copy-start.2 = (f32[64,2048]{1,0:T(8,128)S(1)}, f32[64,2048]{1,0:T(8,128)}, u32[]{:S(2)}) copy-start(f32[64,2048]{1,0:T(8,128)} %reduce-scatter.2.cloned.1.call-done) | copy-start | bytes 1572868
Sparse Core Ops, SparseCore 0:
  9.1 27.6 all-gather.1
  184.2 86.0 reduce-scatter.1
